TPU v7x, 32 devices: a whole 2x2x4 slice. The times are simulated.
32 devices in a mesh: tm: 4 (over y, x), seq: 8 (over z, core).
Axes of the slice: x: 2, y: 2, z: 4, core: 2. Of those that a mesh axis runs over, the one named last changes fastest.
Arguments:
- queries: bfloat16 [4, 1024, 1024], P('tm', 'seq'), may hold values from -5 to 5
- keys: bfloat16 [4, 1024, 1024], P('tm', 'seq'), may hold values from -5 to 5
- values: bfloat16 [4, 1024, 1024], P('tm', 'seq'), may hold values from -6 to 6
- grad_out: bfloat16 [4, 1024, 1024], P('tm', 'seq'), may hold values from -6 to 6
- block_mask: int32 [4, 8, 6], P('tm', 'seq'), may hold values from 0 to 1, as said below
- valid_len: int32 [4], replicated, may hold values from 512 to 1024, as said below
Outputs:
- grad_query: bfloat16 [4, 1024, 1024], P('tm', 'seq')
- grad_key: bfloat16 [4, 1024, 1024], P('tm', 'seq')
- grad_value: bfloat16 [4, 1024, 1024], P('tm', 'seq')
Inputs may be any that keep to these rules, and one draw needn't show every extreme that they name: `block_mask`: entry 1 (a query block's own block) is always 1. `valid_len`: some frame is complete.
All inputs are finite; a program needn't handle non-finite values.
Results may differ from a plain program's by a relative error of at most 0.022.
Values may be sent and summed in bfloat16 or wider, within the bound.
A program may use at most 64 MiB of HBM per device.

v0:
```python
import jax
import jax.numpy as jnp
from jax import lax
from jax.sharding import PartitionSpec as P

HEADS = 8


def extended_2(block, sides, width):
    for axis, dim in sides:
        count = lax.axis_size(axis)
        forward = [(i, i + 1) for i in range(count - 1)]
        backward = [(target, source) for source, target in forward]
        low = lax.ppermute(
            lax.slice_in_dim(block, block.shape[dim] - width, None, axis=dim), axis, forward
        )
        high = lax.ppermute(lax.slice_in_dim(block, 0, width, axis=dim), axis, backward)
        block = jnp.concatenate([low, block, high], axis=dim)
    return block


def shifted(shard, axis, by):
    peers = lax.axis_size(axis)
    pairs = [(i, i + by) for i in range(peers) if 0 <= i + by < peers]
    return lax.ppermute(shard, axis, pairs)


def body(queries, keys, values, grad_out, block_mask, valid_len):
    frames_dev, block_len, feat_dim = queries.shape
    head_dim = feat_dim // HEADS
    scaling = head_dim ** (-0.5)
    seq_pos = lax.axis_index("seq")
    blocks_all = lax.axis_size("seq")
    frame_ids = lax.axis_index("tm") * frames_dev + jnp.arange(frames_dev, dtype=jnp.int32)
    table = jnp.arange(valid_len.shape[0], dtype=jnp.int32)

    def lookup(frame_arr):
        return jnp.sum(jnp.where(frame_arr[..., None] == table, valid_len, 0), axis=-1)

    key_value = jnp.stack((keys, values), 0)
    rimmed = extended_2(key_value, (("seq", 2),), block_len)
    last_frame = shifted(rimmed[:, frames_dev - 1], "tm", 1)
    before = jnp.concatenate((last_frame[:, None], rimmed[:, : frames_dev - 1]), axis=1)
    extended = jnp.concatenate((rimmed, before), axis=2)
    key_heads = extended[0].reshape(frames_dev, 6 * block_len, HEADS, head_dim)
    value_heads = extended[1].reshape(frames_dev, 6 * block_len, HEADS, head_dim)
    candidate = jnp.arange(6, dtype=jnp.int32)
    inside = jnp.arange(block_len, dtype=jnp.int32)
    near_block = seq_pos + candidate % 3 - 1
    src_frame = frame_ids[:, None] - (candidate // 3)[None, :]
    src_valid = lookup(src_frame)
    positions = near_block[:, None] * block_len + inside[None, :]
    block_ok = (
        (block_mask[:, 0, :] == 1)
        & ((near_block >= 0) & (near_block < blocks_all))[None, :]
        & (src_frame >= 0)
    )
    allowed = (block_ok[:, :, None] & (positions[None] < src_valid[:, :, None])).reshape(
        frames_dev, 6 * block_len
    )
    own_valid = lookup(frame_ids)
    query_ok = (seq_pos * block_len + inside)[None, :] < own_valid[:, None]
    query_heads = queries.reshape(frames_dev, block_len, HEADS, head_dim)
    bias = jnp.where(allowed, 0.0, -1e30).astype(jnp.float32)[:, None, None, :]
    masked = (
        jnp.einsum("fihd,fjhd->fhij", query_heads, key_heads, preferred_element_type=jnp.float32)
        * scaling
        + bias
    )
    row_max = jnp.max(masked, axis=-1, keepdims=True)
    log_total = row_max + jnp.log(jnp.sum(jnp.exp(masked - row_max), axis=-1, keepdims=True))
    prob_f32 = jnp.exp(masked - log_total)
    prob_bf = prob_f32.astype(jnp.bfloat16)
    attended = jnp.einsum(
        "fhij,fjhd->fihd", prob_bf, value_heads, preferred_element_type=jnp.float32
    )
    okay = query_ok.astype(jnp.float32)[:, :, None, None]
    attended_bf = (attended * okay).astype(jnp.bfloat16)
    grad_in = (grad_out * query_ok.astype(jnp.bfloat16)[:, :, None]).reshape(
        frames_dev, block_len, HEADS, head_dim
    )
    row_dot = jnp.sum(grad_in.astype(jnp.float32) * attended_bf.astype(jnp.float32), axis=-1)
    dprob = jnp.einsum("fihd,fjhd->fhij", grad_in, value_heads, preferred_element_type=jnp.float32)
    dscore = (prob_f32 * (dprob - jnp.swapaxes(row_dot, 1, 2)[:, :, :, None])).astype(jnp.bfloat16)
    grad_query = scaling * jnp.einsum(
        "fhij,fjhd->fihd", dscore, key_heads, preferred_element_type=jnp.float32
    )
    grad_query = grad_query.astype(jnp.bfloat16).reshape(frames_dev, block_len, feat_dim)
    lse_rows = log_total[..., 0]
    dot_rows = jnp.swapaxes(row_dot, 1, 2)
    mask_vals = block_mask[:, 0, :].astype(jnp.float32)
    slots = jnp.arange(block_len, dtype=jnp.int32)
    gate_rows = jnp.sum(
        jnp.where(slots[None, :, None] == candidate[None, None, :], mask_vals[:, None, :], 0.0),
        axis=-1,
    )
    gate_slab = jnp.broadcast_to(gate_rows[:, None, :], lse_rows.shape)
    stats = jnp.stack((lse_rows, dot_rows, gate_slab), 0)
    query_pack = jnp.stack((queries, grad_in.reshape(frames_dev, block_len, feat_dim)), 0)
    query_rim = extended_2(query_pack, (("seq", 2),), block_len)
    stat_rim = extended_2(stats, (("seq", 3),), block_len)
    next_query = shifted(query_rim[:, 0], "tm", -1)
    next_stat = shifted(stat_rim[:, 0], "tm", -1)
    later_query = jnp.concatenate((query_rim[:, 1:], next_query[:, None]), axis=1)
    later_stat = jnp.concatenate((stat_rim[:, 1:], next_stat[:, None]), axis=1)
    seen_query = jnp.concatenate((query_rim, later_query), axis=2)
    seen_stat = jnp.concatenate((stat_rim, later_stat), axis=3)
    slab = seen_stat[2, :, 0].reshape(frames_dev, 6, block_len)
    pick = 3 * (candidate // 3) + 2 - candidate % 3
    gate = jnp.sum(jnp.where(slots[None, None, :] == pick[None, :, None], slab, 0.0), axis=-1) > 0.5
    key_ok = (seq_pos * block_len + inside)[None, :] < own_valid[:, None]
    permit = jnp.broadcast_to(
        gate[:, :, None, None] & key_ok[:, None, None, :], (frames_dev, 6, block_len, block_len)
    ).reshape(frames_dev, 6 * block_len, block_len)
    in_query = seen_query[0].reshape(frames_dev, 6 * block_len, HEADS, head_dim)
    in_grad = seen_query[1].reshape(frames_dev, 6 * block_len, HEADS, head_dim)
    own_keys = keys.reshape(frames_dev, block_len, HEADS, head_dim)
    own_values = values.reshape(frames_dev, block_len, HEADS, head_dim)
    back_scores = (
        jnp.einsum("fihd,fjhd->fhij", in_query, own_keys, preferred_element_type=jnp.float32)
        * scaling
    )
    back_prob = jnp.where(permit[:, None], jnp.exp(back_scores - seen_stat[0][..., None]), 0.0)
    back_bf = back_prob.astype(jnp.bfloat16)
    back_dprob = jnp.einsum(
        "fihd,fjhd->fhij", in_grad, own_values, preferred_element_type=jnp.float32
    )
    back_dscore = (back_prob * (back_dprob - seen_stat[1][..., None])).astype(jnp.bfloat16)
    grad_key = scaling * jnp.einsum(
        "fhij,fihd->fjhd", back_dscore, in_query, preferred_element_type=jnp.float32
    )
    grad_value = jnp.einsum("fhij,fihd->fjhd", back_bf, in_grad, preferred_element_type=jnp.float32)
    grad_key = grad_key.reshape(frames_dev, block_len, feat_dim).astype(jnp.bfloat16)
    grad_value = grad_value.reshape(frames_dev, block_len, feat_dim).astype(jnp.bfloat16)
    return (grad_query, grad_key, grad_value)


def solution(mesh):
    in_specs = (
        P("tm", "seq", None),
        P("tm", "seq", None),
        P("tm", "seq", None),
        P("tm", "seq", None),
        P("tm", "seq", None),
        P(),
    )
    out_specs = (P("tm", "seq", None), P("tm", "seq", None), P("tm", "seq", None))
    return jax.shard_map(body, mesh=mesh, in_specs=in_specs, out_specs=out_specs, check_vma=False)
```

profile of v0, /device:TPU:1, one launch (start us, length us, event | category | flops | bytes accessed | tf_op | source)
XLA Modules:
  0.0 116.4 jit_solution(7345207568539659828)
XLA Ops:
  0.6 0.0 copy-start.5
  0.7 1.2 %copy.86 = bf16[1,128,1024]{1,2,0:T(8,128)(2,1)S(1)} copy(bf16[1,128,1024]{2,1,0:T(8,128)(2,1)} %param.8) | data formatting | bytes 524288 | tf_op args[2]
  1.8 1.1 copy.85
  3.0 0.9 fusion.72
  3.8 1.9 %collective-permute-start.1 = (bf16[2,1,128,1024]{2,3,0,1:T(8,128)(2,1)}, bf16[2,1,128,1024]{2,3,0,1:T(8,128)(2,1)S(1)}, u32[]{:S(2)}, u32[]{:S(2)}) collective-permute-start(bf16[2,1,128,1024]{2,3,0,1:T(8,128)(2,1)} %get-tuple-element.24), channel_id=1, source_target_pairs={{1,0},{2,1},{3,2},{4,3},{5,4},{6,5},{7,6},{9,8},{10,9},{11,10},{12... | collective-permute-start | bytes 1572872 | tf_op jit(solution)/shard_map/ppermute | solution.py:17
  5.7 4.6 %collective-permute-start = (bf16[2,1,128,1024]{2,3,0,1:T(8,128)(2,1)}, bf16[2,1,128,1024]{2,3,0,1:T(8,128)(2,1)S(1)}, u32[]{:S(2)}, u32[]{:S(2)}) collective-permute-start(bf16[2,1,128,1024]{2,3,0,1:T(8,128)(2,1)} %get-tuple-element.24), channel_id=1, source_target_pairs={{0,1},{1,2},{2,3},{3,4},{4,5},{5,6},{6,7},{8,9},{9,10},{10,11},{11... | collective-permute-start | bytes 1572872 | tf_op jit(solution)/shard_map/ppermute | solution.py:14
  10.3 1.3 %fusion.63 = s32[]{:T(128)} fusion(s32[4]{0:T(128)} %param.11, s32[]{:T(128)S(6)} %axis_index.25), kind=kLoop, calls=%fused_computation.79 | loop fusion | flops 11 | bytes 24 | tf_op jit(solution)/shard_map/reduce_sum | solution.py:38
  11.6 0.7 fusion.73
  12.3 1.1 copy.92
  13.5 0.2 copy.98
  13.7 0.0 copy-start.9
  13.7 0.0 copy-start.10
  13.7 0.9 fusion.71
  14.6 1.9 %collective-permute-start.4 = (bf16[2,1,128,1024]{2,3,0,1:T(8,128)(2,1)S(1)}, bf16[2,1,128,1024]{2,3,0,1:T(8,128)(2,1)S(1)}, u32[]{:S(2)}, u32[]{:S(2)}) collective-permute-start(bf16[2,1,128,1024]{2,3,0,1:T(8,128)(2,1)S(1)} %get-tuple-element.22), channel_id=1, source_target_pairs={{1,0},{2,1},{3,2},{4,3},{5,4},{6,5},{7,6},{9,8},{10,9},{11,10},{12... | collective-permute-start | bytes 1572872 | tf_op jit(solution)/shard_map/ppermute | solution.py:17
  16.5 3.6 %collective-permute-start.3 = (bf16[2,1,128,1024]{2,3,0,1:T(8,128)(2,1)S(1)}, bf16[2,1,128,1024]{2,3,0,1:T(8,128)(2,1)S(1)}, u32[]{:S(2)}, u32[]{:S(2)}) collective-permute-start(bf16[2,1,128,1024]{2,3,0,1:T(8,128)(2,1)S(1)} %get-tuple-element.22), channel_id=1, source_target_pairs={{0,1},{1,2},{2,3},{3,4},{4,5},{5,6},{6,7},{8,9},{9,10},{10,11},{11... | collective-permute-start | bytes 1572872 | tf_op jit(solution)/shard_map/ppermute | solution.py:14
  20.2 1.7 %copy.122 = bf16[16,8,8,128]{3,2,1,0:T(8,128)(2,1)} copy(bf16[16,8,8,128]{3,1,2,0:T(8,128)(2,1)} %bitcast.189) | data formatting | bytes 524288
  22.0 0.2 maximum_bitcast_fusion
  22.2 3.2 %collective-permute-start.2 = (bf16[2,384,1024]{1,2,0:T(8,128)(2,1)S(1)}, bf16[2,384,1024]{1,2,0:T(8,128)(2,1)S(1)}, u32[]{:S(2)}, u32[]{:S(2)}) collective-permute-start(bf16[2,384,1024]{1,2,0:T(8,128)(2,1)S(1)} %maximum_bitcast_fusion), channel_id=1, source_target_pairs={{0,8},{8,16},{16,24},{1,9},{9,17},{17,25},{2,10},{10,18},{18,26},{... | collective-permute-start | bytes 4718600 | tf_op jit(solution)/shard_map/ppermute | solution.py:25
  25.5 0.1 fusion.61
  25.5 0.1 select_reduce_fusion
  25.6 0.1 broadcast_reduce_fusion
  25.8 0.5 add_subtract_fusion
  26.3 0.1 fusion.60
  26.4 0.0 copy-start.6
  26.4 1.5 %maximum_bitcast_fusion.1 = bf16[2,384,1024]{1,2,0:T(8,128)(2,1)} fusion(bf16[2,1,128,1024]{2,3,0,1:T(8,128)(2,1)S(1)} %collective-permute-done.4, bf16[1,1,128,1024]{2,3,0,1:T(8,128)(2,1)S(1)} %fusion.85, bf16[1,1,128,1024]{2,3,0,1:T(8,128)(2,1)S(1)} %bitcast.171, bf16[2,1,128,1024]{2,3,0,1:T(8,128)(2,1)S(1)} %collective-permute-done.3), kind=kLoop, calls=%fused_computation.17 | loop fusion | flops 6291456 | bytes 3145728 | tf_op jit(solution)/shard_map/squeeze | solution.py:102
  27.9 1.3 %collective-permute-start.5 = (bf16[2,384,1024]{1,2,0:T(8,128)(2,1)}, bf16[2,384,1024]{1,2,0:T(8,128)(2,1)}, u32[]{:S(2)}, u32[]{:S(2)}) collective-permute-start(bf16[2,384,1024]{1,2,0:T(8,128)(2,1)} %maximum_bitcast_fusion.1), channel_id=1, source_target_pairs={{8,0},{16,8},{24,16},{9,1},{17,9},{25,17},{10,2},{18,10},{26,18},{... | collective-permute-start | bytes 4718600 | tf_op jit(solution)/shard_map/ppermute | solution.py:25
  29.2 29.5 %collective-permute-done.2 = bf16[2,384,1024]{1,2,0:T(8,128)(2,1)S(1)} collective-permute-done((bf16[2,384,1024]{1,2,0:T(8,128)(2,1)S(1)}, bf16[2,384,1024]{1,2,0:T(8,128)(2,1)S(1)}, u32[]{:S(2)}, u32[]{:S(2)}) %collective-permute-start.2) | collective-permute-done | bytes 1572896 | tf_op jit(solution)/shard_map/ppermute | solution.py:25
  58.8 0.3 pad_maximum_fusion
  59.1 0.2 fusion.75
  59.3 0.9 bitcast_reduce_fusion
  60.3 0.7 fusion.1
  61.0 0.0 copy-done.3
  61.0 1.1 fusion.44
  62.2 1.9 %collective-permute-start.7 = (f32[3,1,8,128]{3,2,0,1:T(8,128)S(1)}, f32[3,1,8,128]{3,2,0,1:T(8,128)S(1)}, u32[]{:S(2)}, u32[]{:S(2)}) collective-permute-start(f32[3,1,8,128]{3,2,0,1:T(8,128)S(1)} %get-tuple-element.28), channel_id=1, source_target_pairs={{1,0},{2,1},{3,2},{4,3},{5,4},{6,5},{7,6},{9,8},{10,9},{11,10},{12... | collective-permute-start | bytes 36872 | tf_op jit(solution)/shard_map/ppermute | solution.py:17
  64.1 3.6 %collective-permute-start.6 = (f32[3,1,8,128]{3,2,0,1:T(8,128)S(1)}, f32[3,1,8,128]{3,2,0,1:T(8,128)S(1)}, u32[]{:S(2)}, u32[]{:S(2)}) collective-permute-start(f32[3,1,8,128]{3,2,0,1:T(8,128)S(1)} %get-tuple-element.28), channel_id=1, source_target_pairs={{0,1},{1,2},{2,3},{3,4},{4,5},{5,6},{6,7},{8,9},{9,10},{10,11},{11... | collective-permute-start | bytes 36872 | tf_op jit(solution)/shard_map/ppermute | solution.py:14
  67.8 4.4 %fusion.27 = bf16[8,128,128]{2,1,0:T(8,128)(2,1)} fusion(bf16[768,8,128]{0,2,1:T(8,128)(2,1)} %bitcast.169, f32[8,768,128]{2,1,0:T(8,128)S(1)} %get-tuple-element.30, bf16[128,8,128]{0,2,1:T(8,128)(2,1)} %bitcast.191, bf16[768,8,128]{0,2,1:T(8,128)(2,1)} %bitcast.184, f32[8,128]{1,0:T(8,128)S(1)} %bitcast.207, f32[8,128]{1,0:T(8,128)S(1)} %log_add_fusion, ...), kind=kOutput, calls=%fused_computation.32 | convolution fusion | flops 407633920 | bytes 6827008 | tf_op jit(solution)/shard_map/fhij,fjhd->fihd/dot_general | solution.py:85
  72.2 22.1 %collective-permute-done.5 = bf16[2,384,1024]{1,2,0:T(8,128)(2,1)} collective-permute-done((bf16[2,384,1024]{1,2,0:T(8,128)(2,1)}, bf16[2,384,1024]{1,2,0:T(8,128)(2,1)}, u32[]{:S(2)}, u32[]{:S(2)}) %collective-permute-start.5) | collective-permute-done | bytes 1572896 | tf_op jit(solution)/shard_map/ppermute | solution.py:25
  94.2 2.0 %pad_maximum_fusion.1 = bf16[2,1,768,1024]{2,3,1,0:T(8,128)(2,1)S(1)} fusion(bf16[2,1,384,1024]{2,3,1,0:T(8,128)(2,1)} %bitcast.29, bf16[2,1,128,1024]{2,3,1,0:T(8,128)(2,1)} %bitcast.176, bf16[2,1,128,1024]{2,3,1,0:T(8,128)(2,1)} %get-tuple-element.21, bf16[2,1,128,1024]{2,3,1,0:T(8,128)(2,1)} %bitcast.177), kind=kLoop, calls=%fused_computation.1 | loop fusion | flops 12582912 | bytes 6291456 | tf_op jit(solution)/shard_map/concatenate | solution.py:106
  96.2 0.2 fusion.74
  96.5 1.3 %collective-permute-start.8 = (f32[3,8,384]{2,1,0:T(8,128)S(1)}, f32[3,8,384]{2,1,0:T(8,128)S(1)}, u32[]{:S(2)}, u32[]{:S(2)}) collective-permute-start(f32[3,8,384]{2,1,0:T(8,128)S(1)} %maximum_bitcast_fusion.2), channel_id=1, source_target_pairs={{8,0},{16,8},{24,16},{9,1},{17,9},{25,17},{10,2},{18,10},{26,18},{... | collective-permute-start | bytes 110600 | tf_op jit(solution)/shard_map/ppermute | solution.py:25
  97.8 2.3 %fusion.53 = f32[8,768,128]{2,1,0:T(8,128)} fusion(bf16[768,8,128]{0,2,1:T(8,128)(2,1)S(1)} %bitcast.166, bf16[128,8,128]{2,1,0:T(8,128)(2,1)S(1)} %bitcast.185), kind=kOutput, calls=%fused_computation.44 | convolution fusion | flops 201326592 | bytes 4980736 | tf_op jit(solution)/shard_map/fihd,fjhd->fhij/dot_general | solution.py:120
  100.1 1.8 %copy.109 = bf16[1,128,1024]{2,1,0:T(8,128)(2,1)} copy(bf16[1,128,1024]{1,2,0:T(8,128)(2,1)} %bitcast.193) | data formatting | bytes 524288
  101.9 0.8 fusion.58
  102.7 0.7 broadcast_and_fusion
  103.5 4.4 %fusion.29 = bf16[8,128,128]{2,1,0:T(8,128)(2,1)} fusion(bf16[768,8,128]{0,2,1:T(8,128)(2,1)S(1)} %bitcast.180, f32[8,768,128]{2,1,0:T(8,128)} %fusion.53, f32[8,768]{1,0:T(8,128)S(1)} %get-tuple-element.25, pred[768,128]{1,0:T(8,128)(4,1)S(1)} %bitcast.202), kind=kOutput, calls=%fused_computation.34 | convolution fusion | flops 204603392 | bytes 5103616 | tf_op jit(solution)/shard_map/fhij,fihd->fjhd/dot_general | solution.py:132
  107.9 4.9 %fusion.28 = bf16[8,128,128]{2,1,0:T(8,128)(2,1)} fusion(bf16[768,8,128]{0,2,1:T(8,128)(2,1)S(1)} %bitcast.167, f32[8,768,128]{2,1,0:T(8,128)} %fusion.53, f32[8,768]{1,0:T(8,128)S(1)} %get-tuple-element.26, f32[8,768]{1,0:T(8,128)S(1)} %get-tuple-element.25, pred[768,128]{1,0:T(8,128)(4,1)S(1)} %bitcast.203, bf16[768,8,128]{0,2,1:T(8,128)(2,1)S(1)} %bitcast.181, ...), kind=kOutput, calls=%fused_computation.33 | convolution fusion | flops 407633920 | bytes 6963200 | tf_op jit(solution)/shard_map/fhij,fihd->fjhd/dot_general | solution.py:129
  112.8 1.8 %copy.110 = bf16[1,128,1024]{2,1,0:T(8,128)(2,1)} copy(bf16[1,128,1024]{1,2,0:T(8,128)(2,1)} %bitcast.195) | data formatting | bytes 524288
  114.6 1.8 %copy.111 = bf16[1,128,1024]{2,1,0:T(8,128)(2,1)} copy(bf16[1,128,1024]{1,2,0:T(8,128)(2,1)} %bitcast.194) | data formatting | bytes 524288
  (41 shorter events, 0.3 us)
Async XLA Ops:
  0.6 19.6 %copy-start.5 = (bf16[1,128,1024]{2,1,0:T(8,128)(2,1)S(1)}, bf16[1,128,1024]{2,1,0:T(8,128)(2,1)}, u32[]{:S(2)}) copy-start(bf16[1,128,1024]{2,1,0:T(8,128)(2,1)} %param.7) | copy-start | bytes 786436
  0.6 12.8 %copy-start.4 = (bf16[1,128,1024]{2,1,0:T(8,128)(2,1)S(1)}, bf16[1,128,1024]{2,1,0:T(8,128)(2,1)}, u32[]{:S(2)}) copy-start(bf16[1,128,1024]{2,1,0:T(8,128)(2,1)} %param.6) | copy-start | bytes 786436
  3.8 18.1 %collective-permute-start.1 = (bf16[2,1,128,1024]{2,3,0,1:T(8,128)(2,1)}, bf16[2,1,128,1024]{2,3,0,1:T(8,128)(2,1)S(1)}, u32[]{:S(2)}, u32[]{:S(2)}) collective-permute-start(bf16[2,1,128,1024]{2,3,0,1:T(8,128)(2,1)} %get-tuple-element.24), channel_id=1, source_target_pairs={{1,0},{2,1},{3,2},{4,3},{5,4},{6,5},{7,6},{9,8},{10,9},{11,10},{12... | collective-permute-start | bytes 1572872 | tf_op jit(solution)/shard_map/ppermute | solution.py:17
  5.7 16.2 %collective-permute-start = (bf16[2,1,128,1024]{2,3,0,1:T(8,128)(2,1)}, bf16[2,1,128,1024]{2,3,0,1:T(8,128)(2,1)S(1)}, u32[]{:S(2)}, u32[]{:S(2)}) collective-permute-start(bf16[2,1,128,1024]{2,3,0,1:T(8,128)(2,1)} %get-tuple-element.24), channel_id=1, source_target_pairs={{0,1},{1,2},{2,3},{3,4},{4,5},{5,6},{6,7},{8,9},{9,10},{10,11},{11... | collective-permute-start | bytes 1572872 | tf_op jit(solution)/shard_map/ppermute | solution.py:14
  12.3 1.1 copy-start.8
  13.7 11.8 %copy-start.9 = (s32[1,1,6]{2,1,0:T(1,128)S(1)}, s32[1,1,6]{2,1,0:T(1,128)}, u32[]{:S(2)}) copy-start(s32[1,1,6]{2,1,0:T(1,128)} %param.10) | copy-start | bytes 76
  13.7 11.9 %copy-start.10 = (s32[4]{0:T(128)S(1)}, s32[4]{0:T(128)}, u32[]{:S(2)}) copy-start(s32[4]{0:T(128)} %param.11) | copy-start | bytes 52
  14.6 11.8 %collective-permute-start.4 = (bf16[2,1,128,1024]{2,3,0,1:T(8,128)(2,1)S(1)}, bf16[2,1,128,1024]{2,3,0,1:T(8,128)(2,1)S(1)}, u32[]{:S(2)}, u32[]{:S(2)}) collective-permute-start(bf16[2,1,128,1024]{2,3,0,1:T(8,128)(2,1)S(1)} %get-tuple-element.22), channel_id=1, source_target_pairs={{1,0},{2,1},{3,2},{4,3},{5,4},{6,5},{7,6},{9,8},{10,9},{11,10},{12... | collective-permute-start | bytes 1572872 | tf_op jit(solution)/shard_map/ppermute | solution.py:17
  16.5 9.9 %collective-permute-start.3 = (bf16[2,1,128,1024]{2,3,0,1:T(8,128)(2,1)S(1)}, bf16[2,1,128,1024]{2,3,0,1:T(8,128)(2,1)S(1)}, u32[]{:S(2)}, u32[]{:S(2)}) collective-permute-start(bf16[2,1,128,1024]{2,3,0,1:T(8,128)(2,1)S(1)} %get-tuple-element.22), channel_id=1, source_target_pairs={{0,1},{1,2},{2,3},{3,4},{4,5},{5,6},{6,7},{8,9},{9,10},{10,11},{11... | collective-permute-start | bytes 1572872 | tf_op jit(solution)/shard_map/ppermute | solution.py:14
  22.2 36.6 %collective-permute-start.2 = (bf16[2,384,1024]{1,2,0:T(8,128)(2,1)S(1)}, bf16[2,384,1024]{1,2,0:T(8,128)(2,1)S(1)}, u32[]{:S(2)}, u32[]{:S(2)}) collective-permute-start(bf16[2,384,1024]{1,2,0:T(8,128)(2,1)S(1)} %maximum_bitcast_fusion), channel_id=1, source_target_pairs={{0,8},{8,16},{16,24},{1,9},{9,17},{17,25},{2,10},{10,18},{18,26},{... | collective-permute-start | bytes 4718600 | tf_op jit(solution)/shard_map/ppermute | solution.py:25
  26.4 34.6 %copy-start.6 = (bf16[1,128,1024]{1,2,0:T(8,128)(2,1)}, bf16[1,128,1024]{1,2,0:T(8,128)(2,1)S(1)}, u32[]{:S(2)}) copy-start(bf16[1,128,1024]{1,2,0:T(8,128)(2,1)S(1)} %broadcast_multiply_fusion) | copy-start | bytes 786436
  26.4 32.4 %copy-start.1 = (bf16[2,1,128,1024]{2,3,0,1:T(8,128)(2,1)}, bf16[2,1,128,1024]{2,3,0,1:T(8,128)(2,1)S(1)}, u32[]{:S(2)}) copy-start(bf16[2,1,128,1024]{2,3,0,1:T(8,128)(2,1)S(1)} %collective-permute-done.4) | copy-start | bytes 1572868
  26.4 32.4 %copy-start.2 = (bf16[2,1,128,1024]{2,3,0,1:T(8,128)(2,1)}, bf16[2,1,128,1024]{2,3,0,1:T(8,128)(2,1)S(1)}, u32[]{:S(2)}) copy-start(bf16[2,1,128,1024]{2,3,0,1:T(8,128)(2,1)S(1)} %collective-permute-done.3) | copy-start | bytes 1572868
  27.9 66.3 %collective-permute-start.5 = (bf16[2,384,1024]{1,2,0:T(8,128)(2,1)}, bf16[2,384,1024]{1,2,0:T(8,128)(2,1)}, u32[]{:S(2)}, u32[]{:S(2)}) collective-permute-start(bf16[2,384,1024]{1,2,0:T(8,128)(2,1)} %maximum_bitcast_fusion.1), channel_id=1, source_target_pairs={{8,0},{16,8},{24,16},{9,1},{17,9},{25,17},{10,2},{18,10},{26,18},{... | collective-permute-start | bytes 4718600 | tf_op jit(solution)/shard_map/ppermute | solution.py:25
  59.3 1.6 %copy-start = (bf16[1,1,768,1024]{2,3,1,0:T(8,128)(2,1)}, bf16[1,1,768,1024]{2,3,1,0:T(8,128)(2,1)S(1)}, u32[]{:S(2)}) copy-start(bf16[1,1,768,1024]{2,3,1,0:T(8,128)(2,1)S(1)} %get-tuple-element.20) | copy-start | bytes 4718596
  59.3 1.7 %copy-start.3 = (bf16[1,1,768,1024]{2,3,1,0:T(8,128)(2,1)}, bf16[1,1,768,1024]{2,3,1,0:T(8,128)(2,1)S(1)}, u32[]{:S(2)}) copy-start(bf16[1,1,768,1024]{2,3,1,0:T(8,128)(2,1)S(1)} %get-tuple-element.19) | copy-start | bytes 4718596
  62.2 34.3 %collective-permute-start.7 = (f32[3,1,8,128]{3,2,0,1:T(8,128)S(1)}, f32[3,1,8,128]{3,2,0,1:T(8,128)S(1)}, u32[]{:S(2)}, u32[]{:S(2)}) collective-permute-start(f32[3,1,8,128]{3,2,0,1:T(8,128)S(1)} %get-tuple-element.28), channel_id=1, source_target_pairs={{1,0},{2,1},{3,2},{4,3},{5,4},{6,5},{7,6},{9,8},{10,9},{11,10},{12... | collective-permute-start | bytes 36872 | tf_op jit(solution)/shard_map/ppermute | solution.py:17
  64.1 32.4 %collective-permute-start.6 = (f32[3,1,8,128]{3,2,0,1:T(8,128)S(1)}, f32[3,1,8,128]{3,2,0,1:T(8,128)S(1)}, u32[]{:S(2)}, u32[]{:S(2)}) collective-permute-start(f32[3,1,8,128]{3,2,0,1:T(8,128)S(1)} %get-tuple-element.28), channel_id=1, source_target_pairs={{0,1},{1,2},{2,3},{3,4},{4,5},{5,6},{6,7},{8,9},{9,10},{10,11},{11... | collective-permute-start | bytes 36872 | tf_op jit(solution)/shard_map/ppermute | solution.py:14
  96.5 5.4 %collective-permute-start.8 = (f32[3,8,384]{2,1,0:T(8,128)S(1)}, f32[3,8,384]{2,1,0:T(8,128)S(1)}, u32[]{:S(2)}, u32[]{:S(2)}) collective-permute-start(f32[3,8,384]{2,1,0:T(8,128)S(1)} %maximum_bitcast_fusion.2), channel_id=1, source_target_pairs={{8,0},{16,8},{24,16},{9,1},{17,9},{25,17},{10,2},{18,10},{26,18},{... | collective-permute-start | bytes 110600 | tf_op jit(solution)/shard_map/ppermute | solution.py:25
  103.5 4.4 %copy-start.7 = (bf16[16,8,8,128]{3,2,1,0:T(8,128)(2,1)S(1)}, bf16[16,8,8,128]{3,2,1,0:T(8,128)(2,1)}, u32[]{:S(2)}) copy-start(bf16[16,8,8,128]{3,2,1,0:T(8,128)(2,1)} %copy.122) | copy-start | bytes 786436
where the time goes:
time: 118 us; the launch traced here: 116 us
  waiting for transfers between devices  51.6 us (44%)
  starting transfers between devices  23.4 us (20%)
  matrix products  18.1 us (15%)
  local copies, waits for them, and re-layouts  11.4 us (10%)
  other arithmetic  10.9 us (9%)
    ppermute x3, waiting for transfers between devices, shifted(): return lax.ppermute(shard, axis, pairs)  51.6 us
    ppermute x3, starting transfers between devices, extended_2(): lax.ppermute(lax.slice_in_dim(block, block.shape[dim] - width, None, axis...  11.9 us
    unnamed x32, local copies, waits for them, and re-layouts  10.8 us
    ppermute x3, starting transfers between devices, shifted(): return lax.ppermute(shard, axis, pairs)  5.79 us
    ppermute x3, starting transfers between devices, extended_2(): lax.ppermute(lax.slice_in_dim(block, 0, width, axis=dim), axis, backward)  5.74 us
    dot_general x1, matrix products, body(): jnp.einsum('fhij,fihd->fjhd', back_dscore, in_query, preferred_element_ty...  4.93 us
    dot_general x1, matrix products, body(): jnp.einsum('fhij,fjhd->fihd', dscore, key_heads, preferred_element_type=j...  4.41 us
    dot_general x1, matrix products, body(): jnp.einsum('fhij,fihd->fjhd', back_bf, in_grad, preferred_element_type=jn...  4.39 us
  transfers between devices with their start and end apart: 9, of which 2 were waited for; matrix products, arithmetic and copies ran while one was open for 19% of the time, Pallas kernels for 0%

commit v1 on v0

v1 whole, which is shorter than its diff:
```python
import functools
import math

import jax
import jax.numpy as jnp
from jax import lax
from jax.experimental import pallas as pl
from jax.experimental.pallas import tpu as pltpu
from jax.sharding import PartitionSpec as P

HEADS = 8
CHUNKS = 4
BIG = 1e30
MESH = pl.DeviceIdType.MESH
SLOT_OF_KIND = (2, 0, 4, 5, 3)
KIND_OF_SLOT = {2: 0, 0: 1, 4: 2, 5: 3, 3: 4}


def kernel(
    frames, blocks, block_len, head_dim,
    k_in, v_in, q_in, g_in, mask_ref, valid_ref,
    dq_ref, dk_ref, dv_ref,
    buf, bias, stat_in, stat_out, local_sem, send_sem, recv_sem, stat_send, stat_recv,
):
    inputs = (k_in, v_in, q_in, g_in)
    t = lax.axis_index("tm")
    s = lax.axis_index("seq")
    per_chunk = HEADS // CHUNKS
    width = per_chunk * head_dim
    scale = head_dim ** (-0.5)
    scale2 = scale * math.log2(math.e)
    has = {-1: s > 0, 1: s < blocks - 1}
    earlier, later = t > 0, t < frames - 1

    def rows(slot):
        return pl.ds(slot * block_len, block_len)

    def cols(c):
        return pl.ds(pl.multiple_of(c * width, width), width)

    def both(*conds):
        out = conds[0]
        for cond in conds[1:]:
            out = jnp.logical_and(out, cond)
        return out

    def copy(k, kind, c):
        slot = SLOT_OF_KIND[kind]
        src = inputs[k].at[0, :, cols(c)] if kind < 3 else buf.at[k, rows(4), cols(c)]
        if kind == 2:
            device = (t + 1, s) if k < 2 else (t - 1, s)
        else:
            device = (t, s - 1) if kind in (0, 3) else (t, s + 1)
        return pltpu.make_async_remote_copy(
            src_ref=src,
            dst_ref=buf.at[k, rows(slot), cols(c)],
            send_sem=send_sem.at[k, kind, c],
            recv_sem=recv_sem.at[k, slot, c],
            device_id=device,
            device_id_type=MESH,
        )

    def sends(k, kind):
        if kind == 2:
            return later if k < 2 else earlier
        side = has[-1] if kind in (0, 3) else has[1]
        if kind < 3:
            return side
        return both(side, earlier if k < 2 else later)

    def arrives(k, slot):
        conds = []
        if slot % 3 == 0:
            conds.append(has[-1])
        if slot % 3 == 2:
            conds.append(has[1])
        if slot >= 3:
            conds.append(earlier if k < 2 else later)
        return both(*conds)

    def stat_copy(f, d, c):
        slot = 3 * f + 1 - d
        return pltpu.make_async_remote_copy(
            src_ref=stat_out.at[slot, c],
            dst_ref=stat_in.at[slot, c],
            send_sem=stat_send.at[slot, c],
            recv_sem=stat_recv.at[slot, c],
            device_id=(t - f, s + d),
            device_id_type=MESH,
        )

    stat_targets = [(0, -1), (0, 1), (1, 0), (1, -1), (1, 1)]

    def stat_sends(f, d):
        conds = []
        if d:
            conds.append(has[d])
        if f:
            conds.append(earlier)
        return both(*conds)

    barrier = pltpu.get_barrier_semaphore()
    expected = jnp.int32(0)
    for dt in (-1, 0, 1):
        for ds in (-1, 0, 1):
            if dt == 0 and ds == 0:
                continue
            conds = []
            if dt:
                conds.append(earlier if dt < 0 else later)
            if ds:
                conds.append(has[ds])
            there = both(*conds)
            expected = expected + there.astype(jnp.int32)

            @pl.when(there)
            def _(dt=dt, ds=ds):
                pl.semaphore_signal(
                    barrier, inc=1, device_id=(t + dt, s + ds), device_id_type=MESH
                )

    own = [
        pltpu.make_async_copy(inputs[k].at[0], buf.at[k, rows(1), :], local_sem.at[k])
        for k in range(4)
    ]
    for c in own:
        c.start()
    pl.semaphore_wait(barrier, expected)

    for group in ((0, 1), (2, 3)):
        @pl.loop(0, CHUNKS)
        def _(c, group=group):
            for kind in (2, 0, 1):
                for k in group:
                    @pl.when(sends(k, kind))
                    def _(k=k, kind=kind):
                        copy(k, kind, c).start()

    for slot in (0, 2, 3, 4, 5):
        for k in range(4):
            @pl.when(jnp.logical_not(arrives(k, slot)))
            def _(k=k, slot=slot):
                buf[k, slot * block_len:(slot + 1) * block_len, :] = jnp.zeros(
                    (block_len, buf.shape[2]), buf.dtype
                )

        @pl.when(jnp.logical_not(arrives(2, slot)))
        def _(slot=slot):
            stat_in[slot] = jnp.full(stat_in.shape[1:], BIG, jnp.float32)

    key_pos = lax.broadcasted_iota(jnp.int32, (block_len, head_dim), 0)
    before = jnp.maximum(t - 1, 0)
    for cand in range(6):
        near = s + cand % 3 - 1
        conds = [jnp.logical_and(near >= 0, near < blocks)]
        frame_valid = valid_ref[t]
        if cand >= 3:
            conds.append(earlier)
            frame_valid = valid_ref[before]
        limit = frame_valid - near * block_len
        chosen = jnp.where(mask_ref[0, 0, cand] == 1, 1, 0) * both(*conds).astype(jnp.int32)
        limit = jnp.maximum(limit, 0) * chosen
        bias[cand * block_len:(cand + 1) * block_len, :] = jnp.where(key_pos < limit, 0.0, -BIG)

    own_limit = valid_ref[t] - s * block_len
    lane = lax.broadcasted_iota(jnp.int32, (1, block_len), 1)
    query_ok = lane < own_limit
    okay = jnp.where(query_ok, 1.0, 0.0)
    for c in own:
        c.wait()

    def relay(c, group):
        for k in group:
            @pl.when(earlier if k < 2 else later)
            def _(k=k):
                copy(k, 2, c).wait_recv()
                for kind in (3, 4):
                    @pl.when(sends(k, kind))
                    def _(kind=kind):
                        copy(k, kind, c).start()

    def await_sides(c, group):
        for slot in (0, 2, 3, 5):
            for k in group:
                @pl.when(arrives(k, slot))
                def _(k=k, slot=slot):
                    copy(k, KIND_OF_SLOT[slot], c).wait_recv()

    own_rows = slice(block_len, 2 * block_len)
    nt = (((1,), (1,)), ((), ()))
    tn = (((0,), (0,)), ((), ()))
    nn = (((1,), (0,)), ((), ()))

    def dot(a, b, dims):
        return lax.dot_general(a, b, dims, preferred_element_type=jnp.float32)

    def forward(c):
        await_sides(c, (0, 1))
        lses, dots = [], []
        for h in range(per_chunk):
            hc = pl.ds(pl.multiple_of(c * width + h * head_dim, head_dim), head_dim)
            key = buf[0, :, hc]
            value = buf[1, :, hc]
            query = buf[2, own_rows, hc]
            grad = buf[3, own_rows, hc]
            score = dot(key, query, nt) * scale2 + bias[...]
            peak = jnp.max(score, axis=0, keepdims=True)
            e = jnp.exp2(score - peak)
            total = jnp.sum(e, axis=0, keepdims=True)
            dprob = dot(value, grad, nt)
            norm = okay / total
            row_dot = jnp.sum(e * dprob, axis=0, keepdims=True) * norm
            dscore = (e * norm * (dprob - row_dot)).astype(jnp.bfloat16)
            dq = dot(dscore, key, tn) * scale
            dq_ref[0, :, hc] = dq.astype(dq_ref.dtype)
            lses.append(jnp.where(query_ok, peak + jnp.log2(total), BIG))
            dots.append(row_dot)
        for f, d in stat_targets + [(0, 0)]:
            slot = 3 * f + 1 - d
            cand = 3 * f + d + 1
            gate = jnp.where(mask_ref[0, 0, cand] == 1, 0.0, BIG)
            dest = stat_in if (f, d) == (0, 0) else stat_out
            for h in range(per_chunk):
                dest[slot, c, h:h + 1, :] = lses[h] + gate
                dest[slot, c, per_chunk + h:per_chunk + h + 1, :] = dots[h]
        for f, d in stat_targets:
            @pl.when(stat_sends(f, d))
            def _(f=f, d=d):
                stat_copy(f, d, c).start()

    @pl.loop(0, CHUNKS + 1)
    def _(c):
        @pl.when(c < CHUNKS)
        def _():
            relay(c, (0, 1))

        @pl.when(c > 0)
        def _():
            forward(c - 1)

        @pl.when(c < CHUNKS)
        def _():
            relay(c, (2, 3))

    key_ok = lax.broadcasted_iota(jnp.int32, (block_len, head_dim), 0) < own_limit

    @pl.loop(0, CHUNKS)
    def _(c):
        await_sides(c, (2, 3))
        for f, d in stat_targets:
            slot = 3 * f + 1 - d

            @pl.when(arrives(2, slot))
            def _(f=f, d=d):
                stat_copy(f, d, c).wait_recv()
        for h in range(per_chunk):
            hc = pl.ds(pl.multiple_of(c * width + h * head_dim, head_dim), head_dim)
            query = buf[2, :, hc]
            grad = buf[3, :, hc]
            key = buf[0, own_rows, hc]
            value = buf[1, own_rows, hc]
            lse = jnp.concatenate([stat_in[j, c, h:h + 1, :] for j in range(6)], axis=1)
            row_dot = jnp.concatenate(
                [stat_in[j, c, per_chunk + h:per_chunk + h + 1, :] for j in range(6)], axis=1
            )
            prob = jnp.exp2(dot(key, query, nt) * scale2 - lse)
            dprob = dot(value, grad, nt)
            dscore = (prob * (dprob - row_dot)).astype(jnp.bfloat16)
            dk = dot(dscore, query, nn) * scale
            dv = dot(prob.astype(jnp.bfloat16), grad, nn)
            dk_ref[0, :, hc] = jnp.where(key_ok, dk, 0.0).astype(dk_ref.dtype)
            dv_ref[0, :, hc] = jnp.where(key_ok, dv, 0.0).astype(dv_ref.dtype)

    @pl.loop(0, CHUNKS)
    def _(c):
        for k in range(4):
            for kind in range(5):
                @pl.when(sends(k, kind))
                def _(k=k, kind=kind):
                    copy(k, kind, c).wait_send()
        for f, d in stat_targets:
            @pl.when(stat_sends(f, d))
            def _(f=f, d=d):
                stat_copy(f, d, c).wait_send()


def solution(mesh):
    frames, blocks = mesh.shape["tm"], mesh.shape["seq"]

    def body(queries, keys, values, grad_out, block_mask, valid_len):
        _, block_len, feat = queries.shape
        out = jax.ShapeDtypeStruct(queries.shape, queries.dtype)
        vmem = pl.BlockSpec(memory_space=pltpu.VMEM)
        smem = pl.BlockSpec(memory_space=pltpu.SMEM)
        hbm = pl.BlockSpec(memory_space=pl.ANY)
        return pl.pallas_call(
            functools.partial(kernel, frames, blocks, block_len, feat // HEADS),
            out_shape=(out, out, out),
            in_specs=[hbm] * 4 + [smem] * 2,
            out_specs=(vmem,) * 3,
            scratch_shapes=[
                pltpu.VMEM((4, 6 * block_len, feat), jnp.bfloat16),
                pltpu.VMEM((6 * block_len, block_len), jnp.float32),
                pltpu.VMEM((6, CHUNKS, 8, block_len), jnp.float32),
                pltpu.VMEM((6, CHUNKS, 8, block_len), jnp.float32),
                pltpu.SemaphoreType.DMA((4,)),
                pltpu.SemaphoreType.DMA((4, 5, CHUNKS)),
                pltpu.SemaphoreType.DMA((4, 6, CHUNKS)),
                pltpu.SemaphoreType.DMA((6, CHUNKS)),
                pltpu.SemaphoreType.DMA((6, CHUNKS)),
            ],
            compiler_params=pltpu.CompilerParams(collective_id=0, has_side_effects=True),
        )(keys, values, queries, grad_out, block_mask, valid_len)

    spec = P("tm", "seq", None)
    return jax.shard_map(
        body, mesh=mesh, in_specs=(spec,) * 5 + (P(),), out_specs=(spec,) * 3, check_vma=False
    )
```

time: 118 us -> 44.1 us (0.37); the launches traced: 116 us -> 43.9 us
  waiting for transfers between devices: 51.6 us -> 0 us
  Pallas kernels: 0 us -> 39.8 us
  starting transfers between devices: 23.4 us -> 0 us
  matrix products: 18.1 us -> 0 us
  other arithmetic: 10.9 us -> 0 us
  local copies, waits for them, and re-layouts: 11.4 us -> 3.46 us
    ppermute x9 -> x0, waiting for transfers between devices: 51.6 us -> none  [the longest x3 51.6 us: shifted(): return lax.ppermute(shard, axis, pairs)]
    pallas_call x0 -> x1, Pallas kernels: none -> 39.8 us  [body(): pl.pallas_call(functools.partial(kernel, frames, blocks, block_len, feat...]
    ppermute x9 -> x0, starting transfers between devices: 23.4 us -> none  [the longest x3 11.9 us: extended_2(): lax.ppermute(lax.slice_in_dim(block, block.shape[dim] - width, None, axis...]
    dot_general x6 -> x0, matrix products: 18.1 us -> none  [the longest x1 4.93 us: body(): jnp.einsum('fhij,fihd->fjhd', back_dscore, in_query, preferred_element_ty...]
    unnamed x32 -> x7, local copies, waits for them, and re-layouts: 10.8 us -> 3.46 us
    reduce_sum x5 -> x0, other arithmetic: 2.94 us -> none  [the longest x2 1.38 us: lookup(): jnp.sum(jnp.where(frame_arr[..., None] == table, valid_len, 0), axis=-1)]
    concatenate x2 -> x0, other arithmetic: 2.32 us -> none  [the longest x1 1.99 us: body(): seen_query = jnp.concatenate((query_rim, later_query), axis=2)]
    another operation x4 -> x0, other arithmetic: 1.77 us -> none  [the longest x2 0.9 us: body(): jnp.stack((queries, grad_in.reshape(frames_dev, block_len, feat_dim)), 0)]
  transfers between devices with their start and end apart: 9 -> 0, of which waited for: 2 -> 0; matrix products, arithmetic and copies ran while one was open for 19% -> 0% of each run, Pallas kernels for 0% -> 0%
where the time goes in v1:
time: 44.1 us; the launch traced here: 43.9 us
  Pallas kernels  39.8 us (90%)
  local copies, waits for them, and re-layouts  3.46 us (8%)
  between operations  0.65 us (1%)
    pallas_call x1, Pallas kernels, body(): pl.pallas_call(functools.partial(kernel, frames, blocks, block_len, feat...  39.8 us
    unnamed x7, local copies, waits for them, and re-layouts  3.46 us

profile of v1, /device:TPU:1, one launch (start us, length us, event | category | flops | bytes accessed | tf_op | source)
XLA Modules:
  0.0 43.9 jit_solution(7602040291939502683)
XLA Ops:
  0.6 39.8 %shard_map.85 = (bf16[1,128,1024]{2,1,0:T(8,128)(2,1)}, bf16[1,128,1024]{2,1,0:T(8,128)(2,1)}, bf16[1,128,1024]{2,1,0:T(8,128)(2,1)}) custom-call(bf16[1,128,1024]{2,1,0:T(8,128)(2,1)} %k_in.1, bf16[1,128,1024]{2,1,0:T(8,128)(2,1)} %v_in.1, bf16[1,128,1024]{2,1,0:T(8,128)(2,1)} %q_in.1, bf16[1,128,1024]{2,1,0:T(8,128)(2,1)} %g_in.1, s32[1,1,6]{2,1,0:T(1,128)} %mask_ref.1, ...), custom_call_target="tpu_custom_call" | custom-call | tf_op jit(solution)/shard_map/pallas_call | solution.py:296
  40.4 0.0 copy-start.1
  40.4 1.7 %copy.12 = bf16[1,128,1024]{2,1,0:T(8,128)(2,1)} copy(bf16[1,128,1024]{2,1,0:T(8,128)(2,1)} %get-tuple-element.6) | data formatting | bytes 524288
  42.1 0.0 copy-done.1
  42.1 0.0 copy-start
  42.1 0.7 %copy.13 = bf16[1,128,1024]{2,1,0:T(8,128)(2,1)} copy(bf16[1,128,1024]{2,1,0:T(8,128)(2,1)S(1)} %copy-done.1) | data formatting | bytes 524288
  42.8 0.3 copy-done
  43.2 0.7 %copy.14 = bf16[1,128,1024]{2,1,0:T(8,128)(2,1)} copy(bf16[1,128,1024]{2,1,0:T(8,128)(2,1)S(1)} %copy-done) | data formatting | bytes 524288
Async XLA Ops:
  40.4 1.7 %copy-start.1 = (bf16[1,128,1024]{2,1,0:T(8,128)(2,1)S(1)}, bf16[1,128,1024]{2,1,0:T(8,128)(2,1)}, u32[]{:S(2)}) copy-start(bf16[1,128,1024]{2,1,0:T(8,128)(2,1)} %get-tuple-element.7) | copy-start | bytes 786436
  42.1 1.0 %copy-start = (bf16[1,128,1024]{2,1,0:T(8,128)(2,1)S(1)}, bf16[1,128,1024]{2,1,0:T(8,128)(2,1)}, u32[]{:S(2)}) copy-start(bf16[1,128,1024]{2,1,0:T(8,128)(2,1)} %get-tuple-element.8) | copy-start | bytes 786436

commit v2 on v1

--- a/solution.py
+++ b/solution.py
@@ -9,7 +9,7 @@
 from jax.sharding import PartitionSpec as P
 
 HEADS = 8
-CHUNKS = 4
+CHUNKS = 2
 BIG = 1e30
 MESH = pl.DeviceIdType.MESH
 SLOT_OF_KIND = (2, 0, 4, 5, 3)
@@ -20,7 +20,7 @@
     frames, blocks, block_len, head_dim,
     k_in, v_in, q_in, g_in, mask_ref, valid_ref,
     dq_ref, dk_ref, dv_ref,
-    buf, bias, stat_in, stat_out, local_sem, send_sem, recv_sem, stat_send, stat_recv,
+    buf, bias, corner, corner_send, corner_recv, stat_in, stat_out, local_sem, send_sem, recv_sem, stat_send, stat_recv,
 ):
     inputs = (k_in, v_in, q_in, g_in)
     t = lax.axis_index("tm")
@@ -60,6 +60,35 @@
             device_id_type=MESH,
         )
 
+    square = frames == 4
+    last = CHUNKS - 1
+
+    def source(k):
+        return t == (1 if k < 2 else 2)
+
+    def at_corner(k):
+        return t == (3 if k < 2 else 0)
+
+    def hop(k):
+        return pltpu.make_async_remote_copy(
+            src_ref=inputs[k].at[0, :, last * width:],
+            dst_ref=corner.at[k % 2],
+            send_sem=send_sem.at[k, 2, last],
+            recv_sem=corner_recv.at[k % 2],
+            device_id=(t + 2, s) if k < 2 else (t - 2, s),
+            device_id_type=MESH,
+        )
+
+    def onward(k):
+        return pltpu.make_async_remote_copy(
+            src_ref=corner.at[k % 2],
+            dst_ref=buf.at[k, rows(4), last * width:],
+            send_sem=corner_send.at[k % 2],
+            recv_sem=recv_sem.at[k, 4, last],
+            device_id=(t - 1, s) if k < 2 else (t + 1, s),
+            device_id_type=MESH,
+        )
+
     def sends(k, kind):
         if kind == 2:
             return later if k < 2 else earlier
@@ -119,6 +148,11 @@
                     barrier, inc=1, device_id=(t + dt, s + ds), device_id_type=MESH
                 )
 
+    if square:
+        opposite = lax.rem(t + 2, frames)
+        pl.semaphore_signal(barrier, inc=1, device_id=(opposite, s), device_id_type=MESH)
+        expected = expected + 1
+
     own = [
         pltpu.make_async_copy(inputs[k].at[0], buf.at[k, rows(1), :], local_sem.at[k])
         for k in range(4)
@@ -127,12 +161,21 @@
         c.start()
     pl.semaphore_wait(barrier, expected)
 
-    for group in ((0, 1), (2, 3)):
+    for group, kinds in (((0, 1, 2, 3), (2,)), ((0, 1), (0, 1)), ((2, 3), (0, 1))):
         @pl.loop(0, CHUNKS)
-        def _(c, group=group):
-            for kind in (2, 0, 1):
+        def _(c, group=group, kinds=kinds):
+            for kind in kinds:
                 for k in group:
-                    @pl.when(sends(k, kind))
+                    there = sends(k, kind)
+                    if kind == 2 and square:
+                        round_corner = both(source(k), c == last)
+                        there = both(there, jnp.logical_not(round_corner))
+
+                        @pl.when(round_corner)
+                        def _(k=k):
+                            hop(k).start()
+
+                    @pl.when(there)
                     def _(k=k, kind=kind):
                         copy(k, kind, c).start()
 
@@ -242,6 +285,14 @@
         def _():
             relay(c, (2, 3))
 
+        if square:
+            for group in ((0, 1), (2, 3)):
+                @pl.when(both(at_corner(group[0]), c == 0))
+                def _(group=group):
+                    for k in group:
+                        hop(k).wait_recv()
+                        onward(k).start()
+
     key_ok = lax.broadcasted_iota(jnp.int32, (block_len, head_dim), 0) < own_limit
 
     @pl.loop(0, CHUNKS)
@@ -282,6 +333,12 @@
             @pl.when(stat_sends(f, d))
             def _(f=f, d=d):
                 stat_copy(f, d, c).wait_send()
+    if square:
+        for group in ((0, 1), (2, 3)):
+            @pl.when(at_corner(group[0]))
+            def _(group=group):
+                for k in group:
+                    onward(k).wait_send()
 
 
 def solution(mesh):
@@ -301,8 +358,11 @@
             scratch_shapes=[
                 pltpu.VMEM((4, 6 * block_len, feat), jnp.bfloat16),
                 pltpu.VMEM((6 * block_len, block_len), jnp.float32),
-                pltpu.VMEM((6, CHUNKS, 8, block_len), jnp.float32),
-                pltpu.VMEM((6, CHUNKS, 8, block_len), jnp.float32),
+                pltpu.VMEM((2, block_len, feat // CHUNKS), jnp.bfloat16),
+                pltpu.SemaphoreType.DMA((2,)),
+                pltpu.SemaphoreType.DMA((2,)),
+                pltpu.VMEM((6, CHUNKS, 16, block_len), jnp.float32),
+                pltpu.VMEM((6, CHUNKS, 16, block_len), jnp.float32),
                 pltpu.SemaphoreType.DMA((4,)),
                 pltpu.SemaphoreType.DMA((4, 5, CHUNKS)),
                 pltpu.SemaphoreType.DMA((4, 6, CHUNKS)),

time: 44.1 us -> 39.5 us (0.90)
  Pallas kernels: 39.8 us -> 35.2 us
    pallas_call x1, Pallas kernels: 39.8 us -> 35.2 us  [body(): pl.pallas_call(functools.partial(kernel, frames, blocks, block_len, feat...]
where the time goes in v2:
time: 39.5 us; the launch traced here: 39.3 us
  Pallas kernels  35.2 us (89%)
  local copies, waits for them, and re-layouts  3.46 us (9%)
  between operations  0.65 us (2%)
    pallas_call x1, Pallas kernels, body(): pl.pallas_call(functools.partial(kernel, frames, blocks, block_len, feat...  35.2 us
    unnamed x7, local copies, waits for them, and re-layouts  3.46 us

profile of v2, /device:TPU:1, one launch (start us, length us, event | category | flops | bytes accessed | tf_op | source)
XLA Modules:
  0.0 39.3 jit_solution(16688533291886906519)
XLA Ops:
  0.6 35.2 %shard_map.85 = (bf16[1,128,1024]{2,1,0:T(8,128)(2,1)}, bf16[1,128,1024]{2,1,0:T(8,128)(2,1)}, bf16[1,128,1024]{2,1,0:T(8,128)(2,1)}) custom-call(bf16[1,128,1024]{2,1,0:T(8,128)(2,1)} %k_in.1, bf16[1,128,1024]{2,1,0:T(8,128)(2,1)} %v_in.1, bf16[1,128,1024]{2,1,0:T(8,128)(2,1)} %q_in.1, bf16[1,128,1024]{2,1,0:T(8,128)(2,1)} %g_in.1, s32[1,1,6]{2,1,0:T(1,128)} %mask_ref.1, ...), custom_call_target="tpu_custom_call" | custom-call | tf_op jit(solution)/shard_map/pallas_call | solution.py:353
  35.8 0.0 copy-start.1
  35.8 1.7 %copy.12 = bf16[1,128,1024]{2,1,0:T(8,128)(2,1)} copy(bf16[1,128,1024]{2,1,0:T(8,128)(2,1)} %get-tuple-element.6) | data formatting | bytes 524288
  37.5 0.0 copy-done.1
  37.5 0.0 copy-start
  37.5 0.7 %copy.13 = bf16[1,128,1024]{2,1,0:T(8,128)(2,1)} copy(bf16[1,128,1024]{2,1,0:T(8,128)(2,1)S(1)} %copy-done.1) | data formatting | bytes 524288
  38.2 0.3 copy-done
  38.6 0.7 %copy.14 = bf16[1,128,1024]{2,1,0:T(8,128)(2,1)} copy(bf16[1,128,1024]{2,1,0:T(8,128)(2,1)S(1)} %copy-done) | data formatting | bytes 524288
Async XLA Ops:
  35.8 1.7 %copy-start.1 = (bf16[1,128,1024]{2,1,0:T(8,128)(2,1)S(1)}, bf16[1,128,1024]{2,1,0:T(8,128)(2,1)}, u32[]{:S(2)}) copy-start(bf16[1,128,1024]{2,1,0:T(8,128)(2,1)} %get-tuple-element.7) | copy-start | bytes 786436
  37.5 1.0 %copy-start = (bf16[1,128,1024]{2,1,0:T(8,128)(2,1)S(1)}, bf16[1,128,1024]{2,1,0:T(8,128)(2,1)}, u32[]{:S(2)}) copy-start(bf16[1,128,1024]{2,1,0:T(8,128)(2,1)} %get-tuple-element.8) | copy-start | bytes 786436
